TPU v7x, 512 devices: a whole 4x4x16 slice. The times are simulated.
512 devices in a mesh: dp: 16 (over z), expert: 32 (over y, x, core).
Axes of the slice: x: 4, y: 4, z: 16, core: 2. Of those that a mesh axis runs over, the one named last changes fastest.
Arguments:
- tokens: bfloat16 [4096, 4096], P('expert', 'dp'), may hold values from -6 to 6
- routing: int32 [4096, 8], P('expert'), may hold values from 0 to 31, all different within a row; in each aligned block of 128 rows (0 to 127, 128 to 255, ...) at most 40 rows name the same one
- gate_probs: float32 [4096, 8], P('expert'), may hold values from 0.05 to 0.3
- paired: int32 [32], P('expert'), may hold values from 0 to 1, as said below
- w_gate: bfloat16 [32, 4096, 768], P('expert', 'dp'), may hold values from -0.09375 to 0.09375
- w_up: bfloat16 [32, 4096, 768], P('expert', 'dp'), may hold values from -0.09375 to 0.09375
- w_down: bfloat16 [32, 768, 4096], P('expert', None, 'dp'), may hold values from -0.21875 to 0.21875
- cotangent: bfloat16 [4096, 4096], P('expert', 'dp'), may hold values from -6 to 6
Outputs:
- output: bfloat16 [4096, 4096], P('expert', 'dp')
- grad_tokens: bfloat16 [4096, 4096], P('expert', 'dp')
- grad_gate: float32 [32, 4096, 768], P('expert', 'dp')
- grad_up: float32 [32, 4096, 768], P('expert', 'dp')
- grad_down: float32 [32, 768, 4096], P('expert', None, 'dp')
Inputs may be any that keep to these rules, and one draw needn't show every extreme that they name: `routing`: each token names 8 different copies; among the tokens of one source (aligned blocks of 128 tokens) no copy is named more than 40 times, a bound that some block reaches. paired[c] equals paired[(c + 16) mod 32]; paired[0] and paired[31] are 1.
All inputs are finite; a program needn't handle non-finite values.
Results may differ from a plain program's by a relative error of at most 0.029.
Values may be sent and summed in bfloat16 or wider, within the bound.
A program may use at most 64 MiB of HBM per device.

v0:
```python
import jax
import jax.numpy as jnp
from jax import lax
from jax.sharding import PartitionSpec as P


def swapped(value, axis, stride):
    mask = 2**stride
    pairs = [(source, source ^ mask) for source in range(lax.axis_size(axis))]
    return lax.ppermute(value, axis, pairs)


def product(left, right):
    return jnp.dot(left, right, preferred_element_type=jnp.float32)


def inner_rows(left, right):
    return lax.dot_general(
        left, right, (((0,), (0,)), ((), ())), preferred_element_type=jnp.float32
    )


def outer_cols(left, right):
    return lax.dot_general(
        left, right, (((1,), (1,)), ((), ())), preferred_element_type=jnp.float32
    )


def rounded(value):
    return lax.optimization_barrier(value.astype(jnp.bfloat16)).astype(jnp.float32)


def per_device(tokens, routing, gate_probs, paired, w_gate, w_up, w_down, cotangent):
    n_expert = lax.axis_size("expert")
    n_data = lax.axis_size("dp")
    token_count, top_count = routing.shape
    slab = tokens.shape[1]
    hidden = w_gate.shape[2]
    capacity = max(2, 5 * token_count * top_count // (4 * n_expert))
    all_rows = n_expert * capacity
    own_rows = all_rows // n_data
    gate_slab = w_gate[0]
    up_slab = w_up[0]
    down_slab = w_down[0]
    flat_route = routing.reshape(token_count * top_count)
    onehot = (flat_route[:, None] == jnp.arange(n_expert, dtype=jnp.int32)[None, :]).astype(
        jnp.int32
    )
    earlier = jnp.cumsum(onehot, axis=0) - onehot
    target = flat_route * capacity + jnp.sum(earlier * onehot, axis=1)
    select = jnp.arange(all_rows, dtype=jnp.int32)[:, None] == target[None, :]
    select_grid = select.reshape(all_rows, token_count, top_count)
    token_select = jnp.any(select_grid, axis=2).astype(jnp.bfloat16)
    weight_select = jnp.sum(select_grid.astype(jnp.float32) * gate_probs[None, :, :], axis=2)
    weight_high = weight_select.astype(jnp.bfloat16)
    weight_low = (weight_select - weight_high.astype(jnp.float32)).astype(jnp.bfloat16)
    send_tokens = product(token_select, tokens).astype(jnp.bfloat16)
    scaled = (gate_probs[:, :, None] * cotangent.astype(jnp.float32)[:, None, :]).astype(
        jnp.bfloat16
    )
    send_grads = product(
        select.astype(jnp.bfloat16), scaled.reshape(token_count * top_count, slab)
    ).astype(jnp.bfloat16)
    arrived = (
        lax.all_to_all(
            send_tokens.reshape(n_expert, capacity, slab),
            "expert",
            split_axis=0,
            concat_axis=0,
            tiled=True,
        ),
        lax.all_to_all(
            send_grads.reshape(n_expert, capacity, slab),
            "expert",
            split_axis=0,
            concat_axis=0,
            tiled=True,
        ),
    )
    token_slab = arrived[0].reshape(all_rows, slab)
    grad_slab = arrived[1].reshape(all_rows, slab)
    block_rows = token_slab
    summed = lax.psum_scatter(
        rounded(
            jnp.concatenate([product(block_rows, gate_slab), product(block_rows, up_slab)], axis=1)
        ).astype(jnp.bfloat16),
        "dp",
        scatter_dimension=0,
        tiled=True,
    ).astype(jnp.float32)
    gate_own = summed[:, :hidden]
    up_own = summed[:, hidden:]
    hid_own = (jax.nn.silu(gate_own) * up_own).astype(jnp.bfloat16)
    piece = lax.all_gather(hid_own, "dp", axis=0, tiled=True)
    answer_acc = product(piece, down_slab)
    grad_down = inner_rows(piece, grad_slab)
    answer_slab = answer_acc.astype(jnp.bfloat16)
    answer_back = lax.all_to_all(
        answer_slab.reshape(n_expert, capacity, slab),
        "expert",
        split_axis=0,
        concat_axis=0,
        tiled=True,
    )
    hidden_parts = (
        outer_cols(grad_slab, down_slab).astype(jnp.bfloat16).reshape(n_data, own_rows, hidden)
    )
    arrived_parts = lax.all_to_all(hidden_parts, "dp", split_axis=0, concat_axis=0, tiled=True)
    grad_hidden = jnp.sum(arrived_parts.astype(jnp.float32), axis=0)
    sigma = jax.nn.sigmoid(gate_own)
    activated = gate_own * sigma
    grad_gate_rows = (grad_hidden * up_own * sigma * (1.0 + gate_own * (1.0 - sigma))).astype(
        jnp.bfloat16
    )
    grad_up_rows = (grad_hidden * activated).astype(jnp.bfloat16)
    piece_gate = lax.all_gather(grad_gate_rows, "dp", axis=0, tiled=True)
    piece_up = lax.all_gather(grad_up_rows, "dp", axis=0, tiled=True)
    block_rows = token_slab
    gate_acc = inner_rows(block_rows, piece_gate)
    up_acc = inner_rows(block_rows, piece_up)
    back_rows = outer_cols(piece_gate, gate_slab) + outer_cols(piece_up, up_slab)
    grad_gate = gate_acc
    grad_up = up_acc
    back_slab = back_rows.astype(jnp.bfloat16)
    back_rows_home = lax.all_to_all(
        back_slab.reshape(n_expert, capacity, slab),
        "expert",
        split_axis=0,
        concat_axis=0,
        tiled=True,
    )
    answer_home = answer_back.reshape(all_rows, slab)
    output = (inner_rows(weight_high, answer_home) + inner_rows(weight_low, answer_home)).astype(
        jnp.bfloat16
    )
    grad_tokens = inner_rows(token_select, back_rows_home.reshape(all_rows, slab)).astype(
        jnp.bfloat16
    )
    other = (
        swapped(grad_gate.astype(jnp.bfloat16), "expert", n_expert.bit_length() - 2).astype(
            grad_gate.dtype
        ),
        swapped(grad_up.astype(jnp.bfloat16), "expert", n_expert.bit_length() - 2).astype(
            grad_up.dtype
        ),
        swapped(grad_down.astype(jnp.bfloat16), "expert", n_expert.bit_length() - 2).astype(
            grad_down.dtype
        ),
    )
    keep = paired.astype(jnp.float32)[0]
    grad_gate = (grad_gate + keep * other[0])[None]
    grad_up = (grad_up + keep * other[1])[None]
    grad_down = (grad_down + keep * other[2])[None]
    return (output, grad_tokens, grad_gate, grad_up, grad_down)


def solution(mesh):
    return jax.shard_map(
        per_device,
        mesh=mesh,
        in_specs=(
            P("expert", "dp"),
            P("expert", None),
            P("expert", None),
            P("expert"),
            P("expert", "dp", None),
            P("expert", "dp", None),
            P("expert", None, "dp"),
            P("expert", "dp"),
        ),
        out_specs=(
            P("expert", "dp"),
            P("expert", "dp"),
            P("expert", "dp", None),
            P("expert", "dp", None),
            P("expert", None, "dp"),
        ),
        check_vma=False,
    )
```

profile of v0, /device:TPU:1, one launch (start us, length us, event | category | flops | bytes accessed | tf_op | source)
XLA Modules:
  0.0 480.7 jit_solution(16176602574999856850)
XLA Ops:
  7.2 0.8 copy.41
  8.2 9.0 %reduce-window.6 = s32[32,8,128]{2,1,0:T(8,128)S(1)} reduce-window(s32[32,8,128]{2,1,0:T(8,128)S(1)} %fusion.24, s32[]{:T(128)} %constant.7.clone.1), window={size=1x1x128 pad=0_0x0_0x127_0}, to_apply=%region_0.0 | reduce-window | flops 4161536 | bytes 262148 | tf_op jit(solution)/shard_map/reduce-window
  17.4 0.1 copy.43
  17.6 0.1 broadcast_add_fusion
  17.9 0.7 multiply_add_fusion.1
  18.6 4.6 fusion
  23.3 2.1 convolution_convert_fusion.4
  25.3 10.4 %all-to-all-start = ((bf16[32,40,256]{2,1,0:T(8,128)(2,1)}), bf16[32,40,256]{2,1,0:T(8,128)(2,1)S(1)}, u32[]{:S(2)}, u32[]{:S(2)}) async-start(bf16[32,40,256]{2,1,0:T(8,128)(2,1)} %bitcast.2), calls=%async_computation | async-start | bytes 1310720 | tf_op jit(solution)/shard_map/all_to_all | solution.py:65
  35.8 0.1 copy.47
  36.0 1.9 fusion.4
  38.0 10.8 %all-to-all-done = bf16[32,40,256]{2,1,0:T(8,128)(2,1)S(1)} async-done(((bf16[32,40,256]{2,1,0:T(8,128)(2,1)}), bf16[32,40,256]{2,1,0:T(8,128)(2,1)S(1)}, u32[]{:S(2)}, u32[]{:S(2)}) %all-to-all-start) | async-done | bytes 655392 | tf_op jit(solution)/shard_map/all_to_all | solution.py:65
  48.8 4.2 all-to-all-start.2
  53.1 0.7 convolution_convert_fusion.1
  53.8 0.7 convolution_convert_fusion.2
  54.5 2.1 pad_maximum_fusion
  56.7 6.3 %copy.48 = bf16[1280,1536]{1,0:T(8,128)(2,1)} copy(bf16[1280,1536]{0,1:T(8,128)(2,1)} %pad_maximum_fusion) | data formatting | bytes 7864320
  63.0 3.0 all-to-all-done.2
  66.1 0.7 convolution_convert_fusion
  66.8 117.4 %all_to_all.25 = bf16[16,80,768]{2,1,0:T(8,128)(2,1)S(1)} all-to-all(bf16[16,80,768]{2,1,0:T(8,128)(2,1)S(1)} %bitcast.77), channel_id=1, replica_groups=mesh['dp'=16,'expert'=32] {'dp'}, dimensions={0} | all-to-all | bytes 3932160 | tf_op jit(solution)/shard_map/all_to_all | solution.py:108
  184.2 0.3 convert_reduce_fusion
  184.5 27.7 %reduce-scatter.4.cloned.1.call-done = bf16[80,1536]{1,0:T(8,128)(2,1)} async-done(((bf16[1280,1536]{1,0:T(8,128)(2,1)}), bf16[80,1536]{1,0:T(8,128)(2,1)}) %reduce-scatter.4.cloned.1.call-update) | async-done | bytes 245776 | tf_op jit(solution)/shard_map/reduce_scatter | solution.py:83
  212.2 1.0 convert_element_type.90
  213.2 0.9 multiply_convert_fusion
  214.1 0.7 all-gather.6.cloned.1.call-update
  214.8 0.2 all-gather.8.cloned.1.call-start
  215.1 0.3 all-gather.8.cloned.1.call-update
  216.1 6.8 %select_reduce_fusion = f32[1280,128]{1,0:T(8,128)S(1)} fusion(f32[128,8]{0,1:T(8,128)S(1)} %copy-done.12, s32[128,8]{0,1:T(8,128)S(1)} %multiply_add_fusion.1), kind=kLoop, calls=%fused_computation.1 | loop fusion | flops 3768320 | bytes 663552 | tf_op jit(solution)/shard_map/reduce_sum | solution.py:54
  222.8 56.5 %all-gather.4.cloned.1.call-done = bf16[1280,768]{1,0:T(8,128)(2,1)} async-done(((bf16[80,768]{1,0:T(8,128)(2,1)}), bf16[1280,768]{1,0:T(8,128)(2,1)}) %all-gather.4.cloned.1.call-update) | async-done | bytes 1966096 | tf_op jit(solution)/shard_map/all_gather | solution.py:94
  279.3 3.1 convolution_convert_fusion.3
  282.4 17.4 %all-to-all-start.1 = ((bf16[32,40,256]{2,1,0:T(8,128)(2,1)}), bf16[32,40,256]{2,1,0:T(8,128)(2,1)S(1)}, u32[]{:S(2)}, u32[]{:S(2)}) async-start(bf16[32,40,256]{2,1,0:T(8,128)(2,1)} %bitcast.7), calls=%async_computation.1 | async-start | bytes 1310720 | tf_op jit(solution)/shard_map/all_to_all | solution.py:98
  299.7 52.7 %all-gather.6.cloned.1.call-done = bf16[1280,768]{1,0:T(8,128)(2,1)} async-done(((bf16[80,768]{1,0:T(8,128)(2,1)}), bf16[1280,768]{1,0:T(8,128)(2,1)}) %all-gather.6.cloned.1.call-update) | async-done | bytes 1966096 | tf_op jit(solution)/shard_map/all_gather | solution.py:116
  352.4 3.0 fusion.25
  355.4 4.6 collective-permute-start
  360.1 64.6 %all-gather.8.cloned.1.call-done = bf16[1280,768]{1,0:T(8,128)(2,1)} async-done(((bf16[80,768]{1,0:T(8,128)(2,1)}), bf16[1280,768]{1,0:T(8,128)(2,1)}) %all-gather.8.cloned.1.call-update) | async-done | bytes 1966096 | tf_op jit(solution)/shard_map/all_gather | solution.py:117
  424.7 2.4 fusion.26
  427.1 4.8 collective-permute-start.1
  431.9 1.7 fusion.27
  433.6 2.3 collective-permute-start.2
  435.9 0.7 fusion.14
  436.6 1.6 fusion.3
  438.2 2.0 add_bitcast_fusion.2
  440.2 1.0 add_bitcast_fusion.1
  441.1 18.0 %all-to-all-start.4 = ((bf16[32,40,256]{2,1,0:T(8,128)(2,1)}), bf16[32,40,256]{2,1,0:T(8,128)(2,1)}, u32[]{:S(2)}, u32[]{:S(2)}) async-start(bf16[32,40,256]{2,1,0:T(8,128)(2,1)} %bitcast.13), calls=%async_computation.4 | async-start | bytes 1310720 | tf_op jit(solution)/shard_map/all_to_all | solution.py:125
  459.1 2.0 add_bitcast_fusion
  461.1 0.3 fusion.19
  461.4 0.9 fusion.5
  462.3 9.8 %all-to-all-done.4 = bf16[32,40,256]{2,1,0:T(8,128)(2,1)} async-done(((bf16[32,40,256]{2,1,0:T(8,128)(2,1)}), bf16[32,40,256]{2,1,0:T(8,128)(2,1)}, u32[]{:S(2)}, u32[]{:S(2)}) %all-to-all-start.4) | async-done | bytes 655392 | tf_op jit(solution)/shard_map/all_to_all | solution.py:125
  472.1 2.1 convolution_convert_fusion.5
  (50 shorter events, 0.9 us)
Async XLA Ops:
  7.2 58.9 %copy-start = (bf16[1,768,256]{2,1,0:T(8,128)(2,1)S(1)}, bf16[1,768,256]{2,1,0:T(8,128)(2,1)}, u32[]{:S(2)}) copy-start(bf16[1,768,256]{2,1,0:T(8,128)(2,1)} %param.14) | copy-start | bytes 1179652
  8.0 27.8 %copy-start.11 = (bf16[128,256]{1,0:T(8,128)(2,1)S(1)}, bf16[128,256]{1,0:T(8,128)(2,1)}, u32[]{:S(2)}) copy-start(bf16[128,256]{1,0:T(8,128)(2,1)} %param.15) | copy-start | bytes 196612
  8.2 27.6 %copy-start.12 = (f32[128,8]{0,1:T(8,128)S(1)}, f32[128,8]{0,1:T(8,128)}, u32[]{:S(2)}) copy-start(f32[128,8]{0,1:T(8,128)} %param.10) | copy-start | bytes 12292
  23.3 2.1 copy-start.9
  25.3 23.5 %all-to-all-start = ((bf16[32,40,256]{2,1,0:T(8,128)(2,1)}), bf16[32,40,256]{2,1,0:T(8,128)(2,1)S(1)}, u32[]{:S(2)}, u32[]{:S(2)}) async-start(bf16[32,40,256]{2,1,0:T(8,128)(2,1)} %bitcast.2), calls=%async_computation | async-start | bytes 1310720 | tf_op jit(solution)/shard_map/all_to_all | solution.py:65
  36.0 17.1 %copy-start.6 = (bf16[1,256,768]{2,1,0:T(8,128)(2,1)S(1)}, bf16[1,256,768]{2,1,0:T(8,128)(2,1)}, u32[]{:S(2)}) copy-start(bf16[1,256,768]{2,1,0:T(8,128)(2,1)} %param.13) | copy-start | bytes 1179652
  48.8 5.0 %copy-start.5 = (bf16[1,256,768]{2,1,0:T(8,128)(2,1)S(1)}, bf16[1,256,768]{2,1,0:T(8,128)(2,1)}, u32[]{:S(2)}) copy-start(bf16[1,256,768]{2,1,0:T(8,128)(2,1)} %param.12) | copy-start | bytes 1179652
  48.8 17.3 %all-to-all-start.2 = ((bf16[32,40,256]{2,1,0:T(8,128)(2,1)}), bf16[32,40,256]{2,1,0:T(8,128)(2,1)S(1)}, u32[]{:S(2)}, u32[]{:S(2)}) async-start(bf16[32,40,256]{2,1,0:T(8,128)(2,1)} %bitcast.10), calls=%async_computation.2 | async-start | bytes 1310720 | tf_op jit(solution)/shard_map/all_to_all | solution.py:72
  53.0 159.2 %reduce-scatter.4.cloned.1.call-start = ((), (), s32[]{:S(2)}) async-start(), calls=%async_computation.9 | async-start | bytes 4177920 | tf_op jit(solution)/shard_map/reduce_scatter | solution.py:83
  63.0 216.3 %all-gather.4.cloned.1.call-start = ((), (), s32[]{:S(2)}) async-start(), calls=%async_computation.6 | async-start | bytes 2088960 | tf_op jit(solution)/shard_map/all_gather | solution.py:94
  66.1 118.1 %copy-start.3 = (bf16[32,40,256]{2,1,0:T(8,128)(2,1)}, bf16[32,40,256]{2,1,0:T(8,128)(2,1)S(1)}, u32[]{:S(2)}) copy-start(bf16[32,40,256]{2,1,0:T(8,128)(2,1)S(1)} %all-to-all-done.2) | copy-start | bytes 1966084
  214.1 138.3 %all-gather.6.cloned.1.call-start = ((), (), s32[]{:S(2)}) async-start(), calls=%async_computation.7 | async-start | bytes 2088960 | tf_op jit(solution)/shard_map/all_gather | solution.py:116
  214.8 209.8 %all-gather.8.cloned.1.call-start = ((), (), s32[]{:S(2)}) async-start(), calls=%async_computation.8 | async-start | bytes 2088960 | tf_op jit(solution)/shard_map/all_gather | solution.py:117
  282.4 158.8 %all-to-all-start.1 = ((bf16[32,40,256]{2,1,0:T(8,128)(2,1)}), bf16[32,40,256]{2,1,0:T(8,128)(2,1)S(1)}, u32[]{:S(2)}, u32[]{:S(2)}) async-start(bf16[32,40,256]{2,1,0:T(8,128)(2,1)} %bitcast.7), calls=%async_computation.1 | async-start | bytes 1310720 | tf_op jit(solution)/shard_map/all_to_all | solution.py:98
  355.4 82.8 %collective-permute-start = (bf16[256,768]{1,0:T(8,128)(2,1)}, bf16[256,768]{1,0:T(8,128)(2,1)}, u32[]{:S(2)}, u32[]{:S(2)}) collective-permute-start(bf16[256,768]{1,0:T(8,128)(2,1)} %get-tuple-element.8), channel_id=1, source_target_pairs={{0,16},{1,17},{2,18},{3,19},{4,20},{5,21},{6,22},{7,23},{8,24},{9,... | collective-permute-start | bytes 1179656 | tf_op jit(solution)/shard_map/ppermute | solution.py:10
  424.7 7.2 %copy-start.4 = (bf16[32,40,256]{2,1,0:T(8,128)(2,1)S(1)}, bf16[32,40,256]{2,1,0:T(8,128)(2,1)}, u32[]{:S(2)}) copy-start(bf16[32,40,256]{2,1,0:T(8,128)(2,1)} %copy-done.3) | copy-start | bytes 1966084
  424.7 7.2 %copy-start.13 = (bf16[1280,768]{1,0:T(8,128)(2,1)S(1)}, bf16[1280,768]{1,0:T(8,128)(2,1)}, u32[]{:S(2)}) copy-start(bf16[1280,768]{1,0:T(8,128)(2,1)} %all-gather.4.cloned.1.call-done) | copy-start | bytes 5898244
  427.1 8.8 %copy-start.1 = (bf16[1280,768]{1,0:T(8,128)(2,1)S(1)}, bf16[1280,768]{1,0:T(8,128)(2,1)}, u32[]{:S(2)}) copy-start(bf16[1280,768]{1,0:T(8,128)(2,1)} %all-gather.6.cloned.1.call-done) | copy-start | bytes 5898244
  427.1 13.1 %collective-permute-start.1 = (bf16[256,768]{1,0:T(8,128)(2,1)S(1)}, bf16[256,768]{1,0:T(8,128)(2,1)S(1)}, u32[]{:S(2)}, u32[]{:S(2)}) collective-permute-start(bf16[256,768]{1,0:T(8,128)(2,1)S(1)} %get-tuple-element.10), channel_id=1, source_target_pairs={{0,16},{1,17},{2,18},{3,19},{4,20},{5,21},{6,22},{7,23},{8,24},{9,... | collective-permute-start | bytes 1179656 | tf_op jit(solution)/shard_map/ppermute | solution.py:10
  433.6 3.0 copy-start.2
  433.6 3.0 copy-start.7
  433.6 25.5 %collective-permute-start.2 = (bf16[768,256]{1,0:T(8,128)(2,1)}, bf16[768,256]{1,0:T(8,128)(2,1)}, u32[]{:S(2)}, u32[]{:S(2)}) collective-permute-start(bf16[768,256]{1,0:T(8,128)(2,1)} %get-tuple-element.12), channel_id=1, source_target_pairs={{0,16},{1,17},{2,18},{3,19},{4,20},{5,21},{6,22},{7,23},{8,24},{9,... | collective-permute-start | bytes 1179656 | tf_op jit(solution)/shard_map/ppermute | solution.py:10
  440.2 19.0 %copy-start.8 = (f32[768,256]{1,0:T(8,128)S(1)}, f32[768,256]{1,0:T(8,128)}, u32[]{:S(2)}) copy-start(f32[768,256]{1,0:T(8,128)} %get-tuple-element.13) | copy-start | bytes 2359300
  441.1 30.9 %all-to-all-start.4 = ((bf16[32,40,256]{2,1,0:T(8,128)(2,1)}), bf16[32,40,256]{2,1,0:T(8,128)(2,1)}, u32[]{:S(2)}, u32[]{:S(2)}) async-start(bf16[32,40,256]{2,1,0:T(8,128)(2,1)} %bitcast.13), calls=%async_computation.4 | async-start | bytes 1310720 | tf_op jit(solution)/shard_map/all_to_all | solution.py:125
  461.1 11.0 %copy-start.10 = (pred[1280,128]{1,0:T(8,128)(4,1)S(1)}, pred[1280,128]{1,0:T(8,128)(4,1)}, u32[]{:S(2)}) copy-start(pred[1280,128]{1,0:T(8,128)(4,1)} %copy-done.9) | copy-start | bytes 491524
Sparse Core Ops, SparseCore 0:
  63.1 149.0 reduce-scatter.3
  214.5 64.7 all-gather.3
  282.1 70.2 all-gather.5
  355.2 69.4 all-gather.7
where the time goes:
time: 482 us; the launch traced here: 481 us
  waiting for transfers between devices  226 us (47%)
  blocking collectives  117 us (24%)
  starting transfers between devices  62 us (13%)
  other arithmetic  30.5 us (6%)
  matrix products  22 us (5%)
  between operations  14.7 us (3%)
  local copies, waits for them, and re-layouts  7.99 us (2%)
    all_to_all x1, blocking collectives, per_device(): lax.all_to_all(hidden_parts, 'dp', split_axis=0, concat_axis=0, tiled=True)  117 us
    all_gather x1, waiting for transfers between devices, per_device(): piece_up = lax.all_gather(grad_up_rows, 'dp', axis=0, tiled=True)  64.6 us
    all_gather x1, waiting for transfers between devices, per_device(): piece = lax.all_gather(hid_own, 'dp', axis=0, tiled=True)  56.5 us
    all_gather x1, waiting for transfers between devices, per_device(): piece_gate = lax.all_gather(grad_gate_rows, 'dp', axis=0, tiled=True)  52.7 us
    reduce_scatter x1, waiting for transfers between devices, per_device(): lax.psum_scatter(rounded(jnp.concatenate([product(block_rows, gate_slab),...  27.7 us
    all_to_all x1, starting transfers between devices, per_device(): lax.all_to_all(back_slab.reshape(n_expert, capacity, slab), 'expert', spl...  18 us
    all_to_all x1, starting transfers between devices, per_device(): lax.all_to_all(answer_slab.reshape(n_expert, capacity, slab), 'expert', s...  17.4 us
    ppermute x3, starting transfers between devices, swapped(): return lax.ppermute(value, axis, pairs)  11.7 us
  transfers between devices with their start and end apart: 11, of which 7 were waited for; matrix products, arithmetic and copies ran while one was open for 8% of the time, Pallas kernels for 0%

commit v1 on v0

v1 whole, which is shorter than its diff:
```python
import functools

import jax
import jax.numpy as jnp
from jax import lax
from jax.experimental import pallas as pl
from jax.experimental.pallas import tpu as pltpu
from jax.sharding import PartitionSpec as P

F32 = jnp.float32
BF16 = jnp.bfloat16
MESH = pl.DeviceIdType.MESH


def nn(left, right):
    return jnp.dot(left, right, preferred_element_type=F32)


def tn(left, right):
    return lax.dot_general(left, right, (((0,), (0,)), ((), ())), preferred_element_type=F32)


def nt(left, right):
    return lax.dot_general(left, right, (((1,), (1,)), ((), ())), preferred_element_type=F32)


def layer(
    n,
    n_exp,
    cap,
    paired,
    route,
    prob,
    tokens,
    cotangent,
    wg,
    wu,
    wd,
    y,
    gt,
    gg,
    gu,
    gd,
    sel,
    high,
    low,
    row_prob,
    stage_x,
    stage_g,
    land_x,
    land_g,
    xb,
    gb,
    part_gu,
    part_d,
    land_gu,
    land_d,
    own_gu,
    act,
    stage_o,
    stage_b,
    home_o,
    home_b,
    pair_out,
    pair_in,
    x_s,
    x_r,
    g_s,
    g_r,
    o_s,
    o_r,
    b_s,
    b_r,
    local_s,
    rs_s,
    rs_r,
    ag_s,
    ag_r,
    pair_s,
    pair_r,
):
    top, count = route.shape
    width, hidden = wg.shape
    rows = n_exp * cap
    own = rows // n
    per = n_exp // n
    half = hidden // 2
    third = hidden // 3
    hops = n // 2
    z = lax.axis_index("dp")
    me = lax.axis_index("expert")
    group = me // per
    left = lax.rem(z + n - 1, n)
    right = lax.rem(z + 1, n)
    partner = lax.rem(me + n_exp // 2, n_exp)

    barrier = pltpu.get_barrier_semaphore()
    for neighbour in (left, right):
        pl.semaphore_signal(
            barrier, inc=1, device_id={"dp": neighbour}, device_id_type=MESH
        )

    @pl.loop(1, n_exp)
    def _(o):
        pl.semaphore_signal(
            barrier, inc=1, device_id={"expert": me ^ o}, device_id_type=MESH
        )

    def chunk(index):
        return pl.ds(pl.multiple_of(lax.rem(index + 4 * n, n) * own, own), own)

    def flat(value):
        return value.astype(F32).reshape(value.shape[0] * cap, width).astype(BF16)

    def blocks(value):
        return value.reshape(value.shape[0] // cap, cap, width).astype(BF16)

    def place(source, target):
        shift = lax.rem(source // per - target // per + n, n)
        return shift * per + lax.rem(source, per)

    copy_id = lax.broadcasted_iota(jnp.int32, (n_exp, count), 0)
    named = jnp.zeros((n_exp, count), F32)
    weight = jnp.zeros((n_exp, count), F32)
    for k in range(top):
        hit = copy_id == route[k : k + 1, :]
        named = named + jnp.where(hit, 1.0, 0.0)
        weight = weight + jnp.where(hit, prob[k : k + 1, :], 0.0)
    before = lax.broadcasted_iota(jnp.int32, (count, count), 0) < lax.broadcasted_iota(
        jnp.int32, (count, count), 1
    )
    earlier = nn(named.astype(BF16), jnp.where(before, 1.0, 0.0).astype(BF16))
    slot = jnp.where(named > 0.5, earlier, -1.0)
    place_id = lax.broadcasted_iota(jnp.int32, (cap, count), 0).astype(F32)
    for c in range(n_exp):
        hit = place_id == slot[c : c + 1, :]
        weighted = jnp.where(hit, weight[c : c + 1, :], 0.0)
        upper = weighted.astype(BF16)
        at = slice(c * cap, (c + 1) * cap)
        sel[at, :] = jnp.where(hit, 1.0, 0.0).astype(BF16)
        high[at, :] = upper
        low[at, :] = (weighted - upper.astype(F32)).astype(BF16)
        row_prob[at, :] = jnp.sum(weighted, axis=1, keepdims=True)

    parts = 4
    many = n_exp // parts
    size = rows // parts

    def dispatch_copy(stage, dest, send, recv, target):
        return pltpu.make_async_remote_copy(
            src_ref=stage.at[target],
            dst_ref=dest.at[place(me, target)],
            send_sem=send.at[me ^ target],
            recv_sem=recv.at[me ^ target],
            device_id={"expert": target},
            device_id_type=MESH,
        )

    def local_dispatch(stage, dest, index):
        return pltpu.make_async_copy(
            stage.at[me], dest.at[lax.rem(me, per)], local_s.at[index]
        )

    stage_x[...] = blocks(nn(sel[...], tokens[...]))
    pl.semaphore_wait(barrier, n_exp + 1)

    @pl.loop(1, n_exp)
    def _(o):
        dispatch_copy(stage_x, land_x, x_s, x_r, me ^ o).start()

    local_dispatch(stage_x, land_x, 0).start()
    stage_g[...] = blocks(nn(sel[...], cotangent[...]) * row_prob[...])

    @pl.loop(1, n_exp)
    def _(o):
        dispatch_copy(stage_g, land_g, g_s, g_r, me ^ o).start()

    local_dispatch(stage_g, land_g, 1).start()

    @pl.loop(1, n_exp)
    def _(o):
        dispatch_copy(stage_x, land_x, x_s, x_r, me ^ o).wait_recv()

    local_dispatch(stage_x, land_x, 0).wait()

    @pl.loop(0, parts)
    def _(b):
        at = pl.ds(pl.multiple_of(b * size, size), size)
        got = flat(land_x[pl.ds(b * many, many)])
        xb[at, :] = got
        part_gu[at, :hidden] = nn(got, wg[...]).astype(BF16)
        part_gu[at, hidden:] = nn(got, wu[...]).astype(BF16)

    streams = [
        (part_gu, 0, hidden, land_gu, 0),
        (part_gu, hidden, hidden, land_gu, 1),
        (part_d, 0, half, land_d, 0),
        (part_d, half, half, land_d, 1),
    ]
    started = []

    def reach(t, way):
        return hops if (t + way) % 2 == 0 else n - 1 - hops

    def rs_copy(t, way, s):
        part, col, wide, land, slab = streams[t]
        far = reach(t, way)
        dest = z + far - s if way == 0 else z - far + s
        src = part.at[chunk(dest), pl.ds(col, wide)] if s == 0 else land.at[slab, way, s - 1]
        return pltpu.make_async_remote_copy(
            src_ref=src,
            dst_ref=land.at[slab, way, s],
            send_sem=rs_s.at[t, way, s],
            recv_sem=rs_r.at[t, way, s],
            device_id={"dp": right if way == 0 else left},
            device_id_type=MESH,
        )

    def rs_send(t, way, s):
        if s < reach(t, way):
            copy = rs_copy(t, way, s)
            copy.start()
            started.append(copy)

    def rs_step(t, s):
        part, col, wide, land, slab = streams[t]
        for way in range(2):
            far = reach(t, way)
            if s < far:
                rs_copy(t, way, s).wait_recv()
                if s + 1 < far:
                    dest = z + far - 1 - s if way == 0 else z - far + 1 + s
                    mine = part[chunk(dest), col : col + wide].astype(F32)
                    land[slab, way, s] = (land[slab, way, s].astype(F32) + mine).astype(BF16)
                    rs_send(t, way, s + 1)

    def rs_total(t, col, wide):
        part, start, _, land, slab = streams[t]
        total = part[chunk(z), start + col : start + col + wide].astype(F32)
        for way in range(2):
            if reach(t, way):
                total = total + land[slab, way, reach(t, way) - 1, :, col : col + wide].astype(F32)
        return total

    def ag_copy(u, sub, way, s):
        at = z - s if way == 0 else z + s
        view = act.at[u, chunk(at), pl.ds(sub * half, half)]
        return pltpu.make_async_remote_copy(
            src_ref=view,
            dst_ref=view,
            send_sem=ag_s.at[u, sub, way, s],
            recv_sem=ag_r.at[u, sub, way, s],
            device_id={"dp": right if way == 0 else left},
            device_id_type=MESH,
        )

    def ag_recv(u, sub, way, s):
        at = z - 1 - s if way == 0 else z + 1 + s
        view = act.at[u, chunk(at), pl.ds(sub * half, half)]
        return pltpu.make_async_remote_copy(
            src_ref=view,
            dst_ref=view,
            send_sem=ag_s.at[u, sub, way, s],
            recv_sem=ag_r.at[u, sub, way, s],
            device_id={"dp": right if way == 0 else left},
            device_id_type=MESH,
        )

    def ag_send(u, sub, way, s):
        if s < reach(u + sub, way):
            copy = ag_copy(u, sub, way, s)
            copy.start()
            started.append(copy)

    def ag_first(u):
        for sub in range(2):
            for way in range(2):
                ag_send(u, sub, way, 0)

    def ag_step(u, s):
        for sub in range(2):
            for way in range(2):
                if s < reach(u + sub, way):
                    ag_recv(u, sub, way, s).wait_recv()
                    ag_send(u, sub, way, s + 1)

    def arrived(s):
        found = []
        for way in range(2):
            if s < n - 1 - hops:
                found.append(z - 1 - s if way == 0 else z + 1 + s)
        if s == hops - 1:
            found += [z + d for d in range(n - hops, hops + 1)]
        return found

    def home_copy(stage, home, send, recv, source, index):
        return pltpu.make_async_remote_copy(
            src_ref=stage.at[index],
            dst_ref=home.at[me],
            send_sem=send.at[me ^ source],
            recv_sem=recv.at[me ^ source],
            device_id={"expert": source},
            device_id_type=MESH,
        )

    def home_local(stage, home, index):
        return pltpu.make_async_copy(
            stage.at[lax.rem(me, per)], home.at[me], local_s.at[index]
        )

    def go_home(stage, home, send, recv, which, index):
        index = lax.rem(index + 4 * n, n)
        for sub in range(per):
            source = lax.rem(index + group, n) * per + sub

            @pl.when(source != me)
            def _():
                home_copy(stage, home, send, recv, source, index * per + sub).start()

            @pl.when(source == me)
            def _():
                home_local(stage, home, which).start()

    def answer(index):
        at = lax.rem(index + 4 * n, n) * per
        stage_o[pl.ds(at, per)] = blocks(nn(act[0, chunk(index), :], wd[...]))
        go_home(stage_o, home_o, o_s, o_r, 2, index)

    def back(index):
        at = lax.rem(index + 4 * n, n) * per
        stage_b[pl.ds(at, per)] = blocks(
            nt(act[1, chunk(index), :], wg[...]) + nt(act[2, chunk(index), :], wu[...])
        )
        go_home(stage_b, home_b, b_s, b_r, 3, index)

    def pair_copy(u, k):
        return pltpu.make_async_remote_copy(
            src_ref=pair_out.at[u, k],
            dst_ref=pair_in.at[u, k],
            send_sem=pair_s.at[u, k],
            recv_sem=pair_r.at[u, k],
            device_id={"expert": partner},
            device_id_type=MESH,
        )

    def weight_grad(u, k):
        cut = slice(k * third, (k + 1) * third)
        if u == 0:
            value = tn(act[0, :, cut], gb[...])
            gd[cut, :] = value
            pair_out[u, k] = value.astype(BF16)
        else:
            value = tn(xb[...], act[u, :, cut])
            (gg if u == 1 else gu)[:, cut] = value
            pair_out[u, k] = value.astype(BF16)
        pair_copy(u, k).start()

    for way in range(2):
        for t in range(2):
            rs_send(t, way, 0)

    @pl.loop(1, n_exp)
    def _(o):
        dispatch_copy(stage_g, land_g, g_s, g_r, me ^ o).wait_recv()

    local_dispatch(stage_g, land_g, 1).wait()

    for s in range(hops):
        for t in range(2):
            rs_step(t, s)
        if s == 0:

            @pl.loop(0, parts)
            def _(b):
                at = pl.ds(pl.multiple_of(b * size, size), size)
                got = flat(land_g[pl.ds(b * many, many)])
                gb[at, :] = got
                part_d[at, :] = nt(got, wd[...]).astype(BF16)

        if s == max(hops - 2, 0):
            for way in range(2):
                for t in range(2, 4):
                    rs_send(t, way, 0)

    step = 128 if half % 128 == 0 else half
    for col in range(0, hidden, step):
        gate = rs_total(0, col, step)
        up = rs_total(1, col, step)
        own_gu[:, col : col + step] = gate
        own_gu[:, hidden + col : hidden + col + step] = up
        act[0, chunk(z), col : col + step] = (gate * jax.nn.sigmoid(gate) * up).astype(BF16)
    ag_first(0)

    for s in range(hops):
        for t in range(2, 4):
            rs_step(t, s)
        if s >= 2:
            ag_step(0, s - 2)
            for index in arrived(s - 2):
                answer(index)
        if s == 1:
            answer(z)

    for col in range(0, hidden, step):
        gate = own_gu[:, col : col + step]
        up = own_gu[:, hidden + col : hidden + col + step]
        t = 2 if col < half else 3
        grad = rs_total(t, col % half, step)
        sigma = jax.nn.sigmoid(gate)
        act[1, chunk(z), col : col + step] = (
            grad * up * sigma * (1.0 + gate * (1.0 - sigma))
        ).astype(BF16)
        act[2, chunk(z), col : col + step] = (grad * (gate * sigma)).astype(BF16)
    ag_first(1)
    for s in range(max(hops - 2, 0), hops):
        ag_step(0, s)
        for index in arrived(s):
            answer(index)
    for s in range(hops):
        ag_step(1, s)
        if s < 3:
            weight_grad(0, s)
        if s == max(hops - 2, 0):
            ag_first(2)
    for k in range(hops, 3):
        weight_grad(0, k)
    back(z)
    for s in range(hops):
        ag_step(2, s)
        for index in arrived(s):
            back(index)
        if s < 3:
            weight_grad(1, s)
    for k in range(hops, 3):
        weight_grad(1, k)
    for k in range(3):
        weight_grad(2, k)

    @pl.loop(1, n_exp)
    def _(o):
        pltpu.make_async_remote_copy(
            src_ref=stage_o.at[place(me ^ o, me)],
            dst_ref=home_o.at[me ^ o],
            send_sem=o_s.at[o],
            recv_sem=o_r.at[o],
            device_id={"expert": me ^ o},
            device_id_type=MESH,
        ).wait()

    home_local(stage_o, home_o, 2).wait()
    got = flat(home_o[...])
    y[...] = (tn(high[...], got) + tn(low[...], got)).astype(BF16)

    @pl.loop(1, n_exp)
    def _(o):
        pltpu.make_async_remote_copy(
            src_ref=stage_b.at[place(me ^ o, me)],
            dst_ref=home_b.at[me ^ o],
            send_sem=b_s.at[o],
            recv_sem=b_r.at[o],
            device_id={"expert": me ^ o},
            device_id_type=MESH,
        ).wait()

    home_local(stage_b, home_b, 3).wait()
    gt[...] = tn(sel[...], flat(home_b[...])).astype(BF16)

    keep = paired[0].astype(F32)
    for u in range(3):
        for k in range(3):
            cut = slice(k * third, (k + 1) * third)
            pair_copy(u, k).wait()
            other = pair_in[u, k].astype(F32) * keep
            if u == 0:
                gd[cut, :] = gd[cut, :] + other
            elif u == 1:
                gg[:, cut] = gg[:, cut] + other
            else:
                gu[:, cut] = gu[:, cut] + other

    for copy in started:
        copy.wait_send()

    @pl.loop(1, n_exp)
    def _(o):
        dispatch_copy(stage_x, land_x, x_s, x_r, me ^ o).wait_send()
        dispatch_copy(stage_g, land_g, g_s, g_r, me ^ o).wait_send()


def per_device(tokens, routing, gate_probs, paired, w_gate, w_up, w_down, cotangent):
    n_exp = lax.axis_size("expert")
    n = lax.axis_size("dp")
    count, top = routing.shape
    width = tokens.shape[1]
    hidden = w_gate.shape[2]
    cap = max(2, 5 * count * top // (4 * n_exp))
    rows = n_exp * cap
    own = rows // n
    half = hidden // 2
    third = hidden // 3
    hops = n // 2
    vmem = pl.BlockSpec(memory_space=pltpu.VMEM)
    dma = pltpu.SemaphoreType.DMA
    outs = pl.pallas_call(
        functools.partial(layer, n, n_exp, cap),
        out_shape=(
            jax.ShapeDtypeStruct((count, width), BF16),
            jax.ShapeDtypeStruct((count, width), BF16),
            jax.ShapeDtypeStruct((width, hidden), F32),
            jax.ShapeDtypeStruct((width, hidden), F32),
            jax.ShapeDtypeStruct((hidden, width), F32),
        ),
        in_specs=[pl.BlockSpec(memory_space=pltpu.SMEM)] + [vmem] * 7,
        out_specs=(vmem,) * 5,
        scratch_shapes=[
            pltpu.VMEM((rows, count), BF16),
            pltpu.VMEM((rows, count), BF16),
            pltpu.VMEM((rows, count), BF16),
            pltpu.VMEM((rows, 1), F32),
            pltpu.VMEM((n_exp, cap, width), BF16),
            pltpu.VMEM((n_exp, cap, width), BF16),
            pltpu.VMEM((n_exp, cap, width), BF16),
            pltpu.VMEM((n_exp, cap, width), BF16),
            pltpu.VMEM((rows, width), BF16),
            pltpu.VMEM((rows, width), BF16),
            pltpu.VMEM((rows, 2 * hidden), BF16),
            pltpu.VMEM((rows, hidden), BF16),
            pltpu.VMEM((2, 2, hops, own, hidden), BF16),
            pltpu.VMEM((2, 2, hops, own, half), BF16),
            pltpu.VMEM((own, 2 * hidden), F32),
            pltpu.VMEM((3, rows, hidden), BF16),
            pltpu.VMEM((n_exp, cap, width), BF16),
            pltpu.VMEM((n_exp, cap, width), BF16),
            pltpu.VMEM((n_exp, cap, width), BF16),
            pltpu.VMEM((n_exp, cap, width), BF16),
            pltpu.VMEM((3, 3, third, width), BF16),
            pltpu.VMEM((3, 3, third, width), BF16),
            dma((n_exp,)),
            dma((n_exp,)),
            dma((n_exp,)),
            dma((n_exp,)),
            dma((n_exp,)),
            dma((n_exp,)),
            dma((n_exp,)),
            dma((n_exp,)),
            dma((4,)),
            dma((4, 2, hops)),
            dma((4, 2, hops)),
            dma((3, 2, 2, hops)),
            dma((3, 2, 2, hops)),
            dma((3, 3)),
            dma((3, 3)),
        ],
        compiler_params=pltpu.CompilerParams(
            collective_id=0, has_side_effects=True, vmem_limit_bytes=56 * 1024 * 1024
        ),
    )(
        paired,
        routing.T,
        gate_probs.T,
        tokens,
        cotangent,
        w_gate[0],
        w_up[0],
        w_down[0],
    )
    y, gt, gg, gu, gd = outs
    return y, gt, gg[None], gu[None], gd[None]


def solution(mesh):
    return jax.shard_map(
        per_device,
        mesh=mesh,
        in_specs=(
            P("expert", "dp"),
            P("expert", None),
            P("expert", None),
            P("expert"),
            P("expert", "dp", None),
            P("expert", "dp", None),
            P("expert", None, "dp"),
            P("expert", "dp"),
        ),
        out_specs=(
            P("expert", "dp"),
            P("expert", "dp"),
            P("expert", "dp", None),
            P("expert", "dp", None),
            P("expert", None, "dp"),
        ),
        check_vma=False,
    )
```

time: 482 us -> 200 us (0.41)
  the two profiles are of different devices: /device:TPU:1 before, /device:TPU:32 now
where the time goes in v1:
time: 200 us; the launch traced here: 199 us
  Pallas kernels  191 us (96%)
  local copies, waits for them, and re-layouts  6.57 us (3%)
    pallas_call x1, Pallas kernels, per_device(): pl.pallas_call(functools.partial(layer, n, n_exp, cap), out_shape=(jax.Sh...  191 us
    unnamed x11, local copies, waits for them, and re-layouts  6.57 us

profile of v1, /device:TPU:32, one launch (start us, length us, event | category | flops | bytes accessed | tf_op | source)
XLA Modules:
  0.0 199.3 jit_solution(6383020896511432700)
XLA Ops:
  1.3 191.5 %shard_map.119 = (bf16[128,256]{1,0:T(8,128)(2,1)}, bf16[128,256]{1,0:T(8,128)(2,1)}, f32[256,768]{1,0:T(8,128)}, f32[256,768]{1,0:T(8,128)}, f32[768,256]{1,0:T(8,128)}) custom-call(s32[1]{0:T(128)S(6)} %copy.18.paired, s32[8,128]{1,0:T(8,128)} %bitcast.14, f32[8,128]{1,0:T(8,128)} %bitcast.15, bf16[128,256]{1,0:T(8,128)(2,1)} %tokens.1, ...), custom_call_target="tpu_custom_call" | custom-call | tf_op jit(solution)/shard_map/pallas_call | solution.py:504
  192.7 0.0 copy-start.2
  192.8 1.5 copy.19
  194.3 0.0 copy-done.2
  194.3 0.6 copy.20
  194.9 0.0 copy-start.1
  194.9 2.1 %copy.21 = f32[1,256,768]{2,1,0:T(8,128)} copy(f32[1,256,768]{2,1,0:T(8,128)} %bitcast.10) | data formatting | bytes 1572864
  197.0 0.0 copy-done.1
  197.0 0.0 copy-start
  197.0 0.9 copy.22
  197.9 0.5 copy-done
  198.4 0.9 copy.23
Async XLA Ops:
  192.7 1.5 copy-start.2
  194.9 2.1 %copy-start.1 = (f32[256,768]{1,0:T(8,128)S(1)}, f32[256,768]{1,0:T(8,128)}, u32[]{:S(2)}) copy-start(f32[256,768]{1,0:T(8,128)} %get-tuple-element.13) | copy-start | bytes 2359300
  197.0 1.4 copy-start

commit v2 on v1

--- a/solution.py
+++ b/solution.py
@@ -10,6 +10,7 @@
 F32 = jnp.float32
 BF16 = jnp.bfloat16
 MESH = pl.DeviceIdType.MESH
+LATE = 2
 
 
 def nn(left, right):
@@ -28,19 +29,22 @@
     n,
     n_exp,
     cap,
-    paired,
+    lag,
+    late,
     route,
     prob,
     tokens,
     cotangent,
+    wg_in,
+    wu_in,
+    wd_in,
+    y,
+    gt,
+    grad_out,
+    pair_got,
     wg,
     wu,
     wd,
-    y,
-    gt,
-    gg,
-    gu,
-    gd,
     sel,
     high,
     low,
@@ -61,6 +65,7 @@
     stage_b,
     home_o,
     home_b,
+    grads,
     pair_out,
     pair_in,
     x_s,
@@ -78,9 +83,12 @@
     ag_r,
     pair_s,
     pair_r,
+    load_s,
+    grad_s,
+    got_s,
 ):
     top, count = route.shape
-    width, hidden = wg.shape
+    width, hidden = wg_in.shape
     rows = n_exp * cap
     own = rows // n
     per = n_exp // n
@@ -105,6 +113,13 @@
         pl.semaphore_signal(
             barrier, inc=1, device_id={"expert": me ^ o}, device_id_type=MESH
         )
+
+    loads = [
+        pltpu.make_async_copy(src, dst, load_s.at[k])
+        for k, (src, dst) in enumerate(((wg_in, wg), (wu_in, wu), (wd_in, wd)))
+    ]
+    for load in loads:
+        load.start()
 
     def chunk(index):
         return pl.ds(pl.multiple_of(lax.rem(index + 4 * n, n) * own, own), own)
@@ -142,17 +157,21 @@
         low[at, :] = (weighted - upper.astype(F32)).astype(BF16)
         row_prob[at, :] = jnp.sum(weighted, axis=1, keepdims=True)
 
-    parts = 4
-    many = n_exp // parts
-    size = rows // parts
-
-    def dispatch_copy(stage, dest, send, recv, target):
+    order = [hops, hops - 1, 1 - hops]
+    later = []
+    for s in range(hops - 1):
+        near = hops - 2 - s
+        later.append([near, -near] if near else [0])
+        order += later[-1]
+    later += [[]] * (hops - len(later))
+
+    def dispatch_copy(stage, dest, send, recv, target, source):
         return pltpu.make_async_remote_copy(
             src_ref=stage.at[target],
-            dst_ref=dest.at[place(me, target)],
-            send_sem=send.at[me ^ target],
-            recv_sem=recv.at[me ^ target],
-            device_id={"expert": target},
+            dst_ref=dest.at[place(source, target)],
+            send_sem=send.at[source ^ target],
+            recv_sem=recv.at[source ^ target],
+            device_id={"expert": target if source is me else source},
             device_id_type=MESH,
         )
 
@@ -161,35 +180,52 @@
             stage.at[me], dest.at[lax.rem(me, per)], local_s.at[index]
         )
 
+    def dispatch(stage, dest, send, recv, which, offsets):
+        for offset in offsets:
+            for sub in range(per):
+                target = lax.rem(group - z - offset + 4 * n, n) * per + sub
+
+                @pl.when(target != me)
+                def _():
+                    dispatch_copy(stage, dest, send, recv, target, me).start()
+
+                @pl.when(target == me)
+                def _():
+                    local_dispatch(stage, dest, which).start()
+
+    def await_chunk(stage, dest, send, recv, which, index):
+        for sub in range(per):
+            source = lax.rem(index + group + 4 * n, n) * per + sub
+
+            @pl.when(source != me)
+            def _():
+                dispatch_copy(stage, dest, send, recv, me, source).wait_recv()
+
+            @pl.when(source == me)
+            def _():
+                local_dispatch(stage, dest, which).wait()
+
+    def fill_x(index):
+        await_chunk(stage_x, land_x, x_s, x_r, 0, index)
+        got = flat(land_x[pl.ds(lax.rem(index + 4 * n, n) * per, per)])
+        xb[chunk(index), :] = got
+        part_gu[chunk(index), :hidden] = nn(got, wg[...]).astype(BF16)
+        part_gu[chunk(index), hidden:] = nn(got, wu[...]).astype(BF16)
+
+    def fill_g(index):
+        await_chunk(stage_g, land_g, g_s, g_r, 1, index)
+        got = flat(land_g[pl.ds(lax.rem(index + 4 * n, n) * per, per)])
+        gb[chunk(index), :] = got
+        part_d[chunk(index), :] = nt(got, wd[...]).astype(BF16)
+
     stage_x[...] = blocks(nn(sel[...], tokens[...]))
     pl.semaphore_wait(barrier, n_exp + 1)
-
-    @pl.loop(1, n_exp)
-    def _(o):
-        dispatch_copy(stage_x, land_x, x_s, x_r, me ^ o).start()
-
-    local_dispatch(stage_x, land_x, 0).start()
+    dispatch(stage_x, land_x, x_s, x_r, 0, order)
     stage_g[...] = blocks(nn(sel[...], cotangent[...]) * row_prob[...])
-
-    @pl.loop(1, n_exp)
-    def _(o):
-        dispatch_copy(stage_g, land_g, g_s, g_r, me ^ o).start()
-
-    local_dispatch(stage_g, land_g, 1).start()
-
-    @pl.loop(1, n_exp)
-    def _(o):
-        dispatch_copy(stage_x, land_x, x_s, x_r, me ^ o).wait_recv()
-
-    local_dispatch(stage_x, land_x, 0).wait()
-
-    @pl.loop(0, parts)
-    def _(b):
-        at = pl.ds(pl.multiple_of(b * size, size), size)
-        got = flat(land_x[pl.ds(b * many, many)])
-        xb[at, :] = got
-        part_gu[at, :hidden] = nn(got, wg[...]).astype(BF16)
-        part_gu[at, hidden:] = nn(got, wu[...]).astype(BF16)
+    for load in loads:
+        load.wait()
+    for offset in order[:3]:
+        fill_x(z + offset)
 
     streams = [
         (part_gu, 0, hidden, land_gu, 0),
@@ -343,96 +379,107 @@
             device_id_type=MESH,
         )
 
+    def grad_copy(u, k):
+        piece = slice(k * third, (k + 1) * third)
+        dest = grad_out[u].at[piece, :] if u == 0 else grad_out[u].at[:, piece]
+        return pltpu.make_async_copy(grads.at[u, k], dest, grad_s.at[u, k])
+
+    def got_copy(u, k):
+        return pltpu.make_async_copy(pair_in.at[u, k], pair_got.at[u, k], got_s.at[u, k])
+
     def weight_grad(u, k):
-        cut = slice(k * third, (k + 1) * third)
+        piece = slice(k * third, (k + 1) * third)
         if u == 0:
-            value = tn(act[0, :, cut], gb[...])
-            gd[cut, :] = value
-            pair_out[u, k] = value.astype(BF16)
+            value = tn(act[0, :, piece], gb[...])
         else:
-            value = tn(xb[...], act[u, :, cut])
-            (gg if u == 1 else gu)[:, cut] = value
-            pair_out[u, k] = value.astype(BF16)
+            value = tn(xb[...], act[u, :, piece])
+        pair_out[u, k] = value.astype(BF16)
         pair_copy(u, k).start()
+        grads[u, k] = value
+        grad_copy(u, k).start()
+
+    step = 128 if half % 128 == 0 else half
+
+    def activate():
+        for col in range(0, hidden, step):
+            gate = rs_total(0, col, step)
+            up = rs_total(1, col, step)
+            own_gu[:, col : col + step] = gate
+            own_gu[:, hidden + col : hidden + col + step] = up
+            act[0, chunk(z), col : col + step] = (gate * jax.nn.sigmoid(gate) * up).astype(BF16)
+
+    def activate_grads():
+        for col in range(0, hidden, step):
+            gate = own_gu[:, col : col + step]
+            up = own_gu[:, hidden + col : hidden + col + step]
+            t = 2 if col < half else 3
+            grad = rs_total(t, col % half, step)
+            sigma = jax.nn.sigmoid(gate)
+            act[1, chunk(z), col : col + step] = (
+                grad * up * sigma * (1.0 + gate * (1.0 - sigma))
+            ).astype(BF16)
+            act[2, chunk(z), col : col + step] = (grad * (gate * sigma)).astype(BF16)
 
     for way in range(2):
         for t in range(2):
             rs_send(t, way, 0)
 
-    @pl.loop(1, n_exp)
-    def _(o):
-        dispatch_copy(stage_g, land_g, g_s, g_r, me ^ o).wait_recv()
-
-    local_dispatch(stage_g, land_g, 1).wait()
-
-    for s in range(hops):
-        for t in range(2):
-            rs_step(t, s)
-        if s == 0:
-
-            @pl.loop(0, parts)
-            def _(b):
-                at = pl.ds(pl.multiple_of(b * size, size), size)
-                got = flat(land_g[pl.ds(b * many, many)])
-                gb[at, :] = got
-                part_d[at, :] = nt(got, wd[...]).astype(BF16)
-
-        if s == max(hops - 2, 0):
+    first_d, first_hid = lag, hops
+    first_gate = lag + hops
+    first_up = first_gate + late
+    pending = []
+    for slot_id in range(first_up + hops):
+        if slot_id < hops:
+            for offset in later[slot_id]:
+                fill_x(z + offset)
+            for t in range(2):
+                rs_step(t, slot_id)
+                cut = 2 * slot_id + t
+                if slot_id < first_d:
+                    ahead = order[cut * n // (2 * first_d) : (cut + 1) * n // (2 * first_d)]
+                    dispatch(stage_g, land_g, g_s, g_r, 1, ahead)
+        s = slot_id - first_d
+        if 0 <= s < hops:
+            for offset in later[s]:
+                fill_g(z + offset)
+            for t in range(2, 4):
+                rs_step(t, s)
+        s = slot_id - first_hid
+        if 0 <= s < hops:
+            ag_step(0, s)
+            for index in arrived(s):
+                answer(index)
+            if s == hops - 1:
+                pending += [(0, k) for k in range(3)]
+        s = slot_id - first_gate
+        if 0 <= s < hops:
+            ag_step(1, s)
+            if s == hops - 1:
+                pending += [(1, k) for k in range(3)]
+        s = slot_id - first_up
+        if 0 <= s < hops:
+            ag_step(2, s)
+            for index in arrived(s):
+                back(index)
+        if slot_id + 1 == first_d:
+            for offset in order[:3]:
+                fill_g(z + offset)
             for way in range(2):
                 for t in range(2, 4):
                     rs_send(t, way, 0)
-
-    step = 128 if half % 128 == 0 else half
-    for col in range(0, hidden, step):
-        gate = rs_total(0, col, step)
-        up = rs_total(1, col, step)
-        own_gu[:, col : col + step] = gate
-        own_gu[:, hidden + col : hidden + col + step] = up
-        act[0, chunk(z), col : col + step] = (gate * jax.nn.sigmoid(gate) * up).astype(BF16)
-    ag_first(0)
-
-    for s in range(hops):
-        for t in range(2, 4):
-            rs_step(t, s)
-        if s >= 2:
-            ag_step(0, s - 2)
-            for index in arrived(s - 2):
-                answer(index)
-        if s == 1:
+        if slot_id + 1 == first_hid:
+            activate()
+            ag_first(0)
             answer(z)
-
-    for col in range(0, hidden, step):
-        gate = own_gu[:, col : col + step]
-        up = own_gu[:, hidden + col : hidden + col + step]
-        t = 2 if col < half else 3
-        grad = rs_total(t, col % half, step)
-        sigma = jax.nn.sigmoid(gate)
-        act[1, chunk(z), col : col + step] = (
-            grad * up * sigma * (1.0 + gate * (1.0 - sigma))
-        ).astype(BF16)
-        act[2, chunk(z), col : col + step] = (grad * (gate * sigma)).astype(BF16)
-    ag_first(1)
-    for s in range(max(hops - 2, 0), hops):
-        ag_step(0, s)
-        for index in arrived(s):
-            answer(index)
-    for s in range(hops):
-        ag_step(1, s)
-        if s < 3:
-            weight_grad(0, s)
-        if s == max(hops - 2, 0):
+        if slot_id + 1 == first_gate:
+            activate_grads()
+            ag_first(1)
+        if slot_id + 1 == first_up:
             ag_first(2)
-    for k in range(hops, 3):
-        weight_grad(0, k)
-    back(z)
-    for s in range(hops):
-        ag_step(2, s)
-        for index in arrived(s):
-            back(index)
-        if s < 3:
-            weight_grad(1, s)
-    for k in range(hops, 3):
-        weight_grad(1, k)
+            back(z)
+        for item in pending:
+            weight_grad(*item)
+        pending = []
     for k in range(3):
         weight_grad(2, k)
 
@@ -465,26 +512,62 @@
     home_local(stage_b, home_b, 3).wait()
     gt[...] = tn(sel[...], flat(home_b[...])).astype(BF16)
 
-    keep = paired[0].astype(F32)
     for u in range(3):
         for k in range(3):
-            cut = slice(k * third, (k + 1) * third)
             pair_copy(u, k).wait()
-            other = pair_in[u, k].astype(F32) * keep
-            if u == 0:
-                gd[cut, :] = gd[cut, :] + other
-            elif u == 1:
-                gg[:, cut] = gg[:, cut] + other
-            else:
-                gu[:, cut] = gu[:, cut] + other
+            got_copy(u, k).start()
+    for u in range(3):
+        for k in range(3):
+            grad_copy(u, k).wait()
+            got_copy(u, k).wait()
 
     for copy in started:
         copy.wait_send()
 
     @pl.loop(1, n_exp)
     def _(o):
-        dispatch_copy(stage_x, land_x, x_s, x_r, me ^ o).wait_send()
-        dispatch_copy(stage_g, land_g, g_s, g_r, me ^ o).wait_send()
+        dispatch_copy(stage_x, land_x, x_s, x_r, me ^ o, me).wait_send()
+        dispatch_copy(stage_g, land_g, g_s, g_r, me ^ o, me).wait_send()
+
+
+def finish(paired, y_in, gt_in, gd_in, gg_in, gu_in, other, y, gt, gd, gg, gu, mine, got, s_pass, s_mine, s_got, s_out):
+    third = other.shape[2]
+    keep = paired[...].astype(F32)
+    moves = [
+        pltpu.make_async_copy(y_in, y, s_pass.at[0]),
+        pltpu.make_async_copy(gt_in, gt, s_pass.at[1]),
+    ]
+
+    def part(ref, u, k):
+        piece = slice(k * third, (k + 1) * third)
+        return ref.at[piece, :] if u == 0 else ref.at[:, piece]
+
+    pieces = [(u, k) for u in range(3) for k in range(3)]
+    ins, outs = (gd_in, gg_in, gu_in), (gd, gg, gu)
+    loads = {}
+    for u, k in pieces:
+        loads[u, k] = (
+            pltpu.make_async_copy(part(ins[u], u, k), mine.at[u, k], s_mine.at[u, k]),
+            pltpu.make_async_copy(other.at[u, k], got.at[u, k], s_got.at[u, k]),
+        )
+        for load in loads[u, k]:
+            load.start()
+    for move in moves:
+        move.start()
+    for u, k in pieces:
+        for load in loads[u, k]:
+            load.wait()
+        mine[u, k] = mine[u, k] + keep * got[u, k].astype(F32)
+        move = pltpu.make_async_copy(mine.at[u, k], part(outs[u], u, k), s_out.at[u, k])
+        move.start()
+        moves.append(move)
+    for move in moves:
+        move.wait()
+
+
+def layer_call(sizes, *refs):
+    refs = list(refs)
+    layer(*sizes, *refs[:9], tuple(refs[9:12]), *refs[12:])
 
 
 def per_device(tokens, routing, gate_probs, paired, w_gate, w_up, w_down, cotangent):
@@ -500,19 +583,25 @@
     third = hidden // 3
     hops = n // 2
     vmem = pl.BlockSpec(memory_space=pltpu.VMEM)
+    hbm = pl.BlockSpec(memory_space=pl.ANY)
     dma = pltpu.SemaphoreType.DMA
+    lag = min(4, max(hops - 1, 1))
     outs = pl.pallas_call(
-        functools.partial(layer, n, n_exp, cap),
+        functools.partial(layer_call, (n, n_exp, cap, lag, LATE)),
         out_shape=(
             jax.ShapeDtypeStruct((count, width), BF16),
             jax.ShapeDtypeStruct((count, width), BF16),
+            jax.ShapeDtypeStruct((hidden, width), F32),
             jax.ShapeDtypeStruct((width, hidden), F32),
             jax.ShapeDtypeStruct((width, hidden), F32),
-            jax.ShapeDtypeStruct((hidden, width), F32),
+            jax.ShapeDtypeStruct((3, 3, third, width), BF16),
         ),
-        in_specs=[pl.BlockSpec(memory_space=pltpu.SMEM)] + [vmem] * 7,
-        out_specs=(vmem,) * 5,
+        in_specs=[vmem] * 4 + [hbm] * 3,
+        out_specs=(vmem, vmem, hbm, hbm, hbm, hbm),
         scratch_shapes=[
+            pltpu.VMEM((width, hidden), BF16),
+            pltpu.VMEM((width, hidden), BF16),
+            pltpu.VMEM((hidden, width), BF16),
             pltpu.VMEM((rows, count), BF16),
             pltpu.VMEM((rows, count), BF16),
             pltpu.VMEM((rows, count), BF16),
@@ -533,6 +622,7 @@
             pltpu.VMEM((n_exp, cap, width), BF16),
             pltpu.VMEM((n_exp, cap, width), BF16),
             pltpu.VMEM((n_exp, cap, width), BF16),
+            pltpu.VMEM((3, 3, third, width), F32),
             pltpu.VMEM((3, 3, third, width), BF16),
             pltpu.VMEM((3, 3, third, width), BF16),
             dma((n_exp,)),
@@ -550,12 +640,14 @@
             dma((3, 2, 2, hops)),
             dma((3, 3)),
             dma((3, 3)),
+            dma((3,)),
+            dma((3, 3)),
+            dma((3, 3)),
         ],
         compiler_params=pltpu.CompilerParams(
             collective_id=0, has_side_effects=True, vmem_limit_bytes=56 * 1024 * 1024
         ),
     )(
-        paired,
         routing.T,
         gate_probs.T,
         tokens,
@@ -564,7 +656,27 @@
         w_up[0],
         w_down[0],
     )
-    y, gt, gg, gu, gd = outs
+    y, gt, gd, gg, gu = pl.pallas_call(
+        finish,
+        out_shape=(
+            jax.ShapeDtypeStruct((count, width), BF16),
+            jax.ShapeDtypeStruct((count, width), BF16),
+            jax.ShapeDtypeStruct((hidden, width), F32),
+            jax.ShapeDtypeStruct((width, hidden), F32),
+            jax.ShapeDtypeStruct((width, hidden), F32),
+        ),
+        in_specs=[vmem] + [hbm] * 6,
+        out_specs=(hbm,) * 5,
+        scratch_shapes=[
+            pltpu.VMEM((3, 3, third, width), F32),
+            pltpu.VMEM((3, 3, third, width), BF16),
+            dma((2,)),
+            dma((3, 3)),
+            dma((3, 3)),
+            dma((3, 3)),
+        ],
+        compiler_params=pltpu.CompilerParams(vmem_limit_bytes=58 * 1024 * 1024),
+    )(paired.reshape(1, 1), *outs)
     return y, gt, gg[None], gu[None], gd[None]
 
 

time: 200 us -> 181 us (0.905)
  the two profiles are of different devices: /device:TPU:32 before, /device:TPU:8 now
where the time goes in v2:
time: 181 us; the launch traced here: 180 us
  Pallas kernels  179 us (99%)
    pallas_call x1, Pallas kernels, per_device(): pl.pallas_call(functools.partial(layer_call, (n, n_exp, cap, lag, LATE)),...  174 us
    pallas_call x1, Pallas kernels, per_device(): pl.pallas_call(finish, out_shape=(jax.ShapeDtypeStruct((count, width), BF...  5.37 us

profile of v2, /device:TPU:8, one launch (start us, length us, event | category | flops | bytes accessed | tf_op | source)
XLA Modules:
  0.0 180.5 jit_solution(5994907990502365799)
XLA Ops:
  1.3 173.6 %shard_map.119 = (bf16[128,256]{1,0:T(8,128)(2,1)}, bf16[128,256]{1,0:T(8,128)(2,1)}, f32[768,256]{1,0:T(8,128)}, f32[256,768]{1,0:T(8,128)}, f32[256,768]{1,0:T(8,128)}, /*index=5*/bf16[3,3,256,256]{3,2,1,0:T(8,128)(2,1)}) custom-call(s32[8,128]{1,0:T(8,128)} %bitcast.13, f32[8,128]{1,0:T(8,128)} %bitcast.14, bf16[128,256]{1,0:T(8,128)(2,1)} %refs_2_.1, ...), custom_call_target="tpu_custom_call" | custom-call | tf_op jit(solution)/shard_map/pallas_call | solution.py:589
  174.9 5.4 %shard_map.120 = (bf16[128,256]{1,0:T(8,128)(2,1)}, bf16[128,256]{1,0:T(8,128)(2,1)}, f32[768,256]{1,0:T(8,128)}, f32[256,768]{1,0:T(8,128)}, f32[256,768]{1,0:T(8,128)}) custom-call(s32[1,1]{1,0:T(1,128)} %bitcast.9.paired, bf16[128,256]{1,0:T(8,128)(2,1)} %get-tuple-element.16.y_in, bf16[128,256]{1,0:T(8,128)(2,1)} %get-tuple-element.17.gt_in, ...), custom_call_target="tpu_custom_call" | custom-call | tf_op jit(solution)/shard_map/pallas_call | solution.py:659

commit v3 on v2

--- a/solution.py
+++ b/solution.py
@@ -10,7 +10,7 @@
 F32 = jnp.float32
 BF16 = jnp.bfloat16
 MESH = pl.DeviceIdType.MESH
-LATE = 2
+LATE = 4
 
 
 def nn(left, right):
@@ -308,10 +308,9 @@
             copy.start()
             started.append(copy)
 
-    def ag_first(u):
-        for sub in range(2):
-            for way in range(2):
-                ag_send(u, sub, way, 0)
+    def ag_first(u, sub):
+        for way in range(2):
+            ag_send(u, sub, way, 0)
 
     def ag_step(u, s):
         for sub in range(2):
@@ -400,20 +399,19 @@
 
     step = 128 if half % 128 == 0 else half
 
-    def activate():
-        for col in range(0, hidden, step):
+    def activate(sub):
+        for col in range(sub * half, (sub + 1) * half, step):
             gate = rs_total(0, col, step)
             up = rs_total(1, col, step)
             own_gu[:, col : col + step] = gate
             own_gu[:, hidden + col : hidden + col + step] = up
             act[0, chunk(z), col : col + step] = (gate * jax.nn.sigmoid(gate) * up).astype(BF16)
 
-    def activate_grads():
-        for col in range(0, hidden, step):
+    def activate_grads(sub):
+        for col in range(sub * half, (sub + 1) * half, step):
             gate = own_gu[:, col : col + step]
             up = own_gu[:, hidden + col : hidden + col + step]
-            t = 2 if col < half else 3
-            grad = rs_total(t, col % half, step)
+            grad = rs_total(2 + sub, col - sub * half, step)
             sigma = jax.nn.sigmoid(gate)
             act[1, chunk(z), col : col + step] = (
                 grad * up * sigma * (1.0 + gate * (1.0 - sigma))
@@ -468,14 +466,17 @@
                 for t in range(2, 4):
                     rs_send(t, way, 0)
         if slot_id + 1 == first_hid:
-            activate()
-            ag_first(0)
+            for sub in range(2):
+                activate(sub)
+                ag_first(0, sub)
             answer(z)
         if slot_id + 1 == first_gate:
-            activate_grads()
-            ag_first(1)
+            for sub in range(2):
+                activate_grads(sub)
+                ag_first(1, sub)
         if slot_id + 1 == first_up:
-            ag_first(2)
+            for sub in range(2):
+                ag_first(2, sub)
             back(z)
         for item in pending:
             weight_grad(*item)
@@ -483,6 +484,12 @@
     for k in range(3):
         weight_grad(2, k)
 
+    def take_pair(u):
+        for k in range(3):
+            pair_copy(u, k).wait()
+            got_copy(u, k).start()
+
+    take_pair(0)
     @pl.loop(1, n_exp)
     def _(o):
         pltpu.make_async_remote_copy(
@@ -512,10 +519,8 @@
     home_local(stage_b, home_b, 3).wait()
     gt[...] = tn(sel[...], flat(home_b[...])).astype(BF16)
 
-    for u in range(3):
-        for k in range(3):
-            pair_copy(u, k).wait()
-            got_copy(u, k).start()
+    for u in range(1, 3):
+        take_pair(u)
     for u in range(3):
         for k in range(3):
             grad_copy(u, k).wait()
@@ -530,39 +535,66 @@
         dispatch_copy(stage_g, land_g, g_s, g_r, me ^ o, me).wait_send()
 
 
-def finish(paired, y_in, gt_in, gd_in, gg_in, gu_in, other, y, gt, gd, gg, gu, mine, got, s_pass, s_mine, s_got, s_out):
+def finish(
+    paired,
+    y_in,
+    gt_in,
+    gd_in,
+    gg_in,
+    gu_in,
+    other,
+    y,
+    gt,
+    gd,
+    gg,
+    gu,
+    small,
+    sum_d,
+    sum_g,
+    sum_u,
+    got,
+    s_in,
+    s_out,
+    s_pass,
+):
     third = other.shape[2]
     keep = paired[...].astype(F32)
-    moves = [
-        pltpu.make_async_copy(y_in, y, s_pass.at[0]),
-        pltpu.make_async_copy(gt_in, gt, s_pass.at[1]),
-    ]
-
-    def part(ref, u, k):
-        piece = slice(k * third, (k + 1) * third)
-        return ref.at[piece, :] if u == 0 else ref.at[:, piece]
-
-    pieces = [(u, k) for u in range(3) for k in range(3)]
-    ins, outs = (gd_in, gg_in, gu_in), (gd, gg, gu)
-    loads = {}
-    for u, k in pieces:
-        loads[u, k] = (
-            pltpu.make_async_copy(part(ins[u], u, k), mine.at[u, k], s_mine.at[u, k]),
-            pltpu.make_async_copy(other.at[u, k], got.at[u, k], s_got.at[u, k]),
-        )
-        for load in loads[u, k]:
+    arrays = ((gd_in, sum_d, gd), (gg_in, sum_g, gg), (gu_in, sum_u, gu))
+    loads = []
+    for u, (src, mine, _) in enumerate(arrays):
+        both = (
+            pltpu.make_async_copy(other.at[u], got.at[u], s_in.at[u, 0]),
+            pltpu.make_async_copy(src, mine, s_in.at[u, 1]),
+        )
+        for load in both:
             load.start()
-    for move in moves:
-        move.start()
-    for u, k in pieces:
-        for load in loads[u, k]:
+        loads.append(both)
+    passed = []
+    for k, ref in enumerate((y_in, gt_in)):
+        load = pltpu.make_async_copy(ref, small.at[k], s_pass.at[0, k])
+        load.start()
+        passed.append(load)
+    stores = []
+    for k, ref in enumerate((y, gt)):
+        passed[k].wait()
+        store = pltpu.make_async_copy(small.at[k], ref, s_pass.at[1, k])
+        store.start()
+        stores.append(store)
+    for u, (_, mine, dst) in enumerate(arrays):
+        for load in loads[u]:
             load.wait()
-        mine[u, k] = mine[u, k] + keep * got[u, k].astype(F32)
-        move = pltpu.make_async_copy(mine.at[u, k], part(outs[u], u, k), s_out.at[u, k])
-        move.start()
-        moves.append(move)
-    for move in moves:
-        move.wait()
+        for k in range(3):
+            piece = slice(k * third, (k + 1) * third)
+            value = keep * got[u, k].astype(F32)
+            if u == 0:
+                mine[piece, :] = mine[piece, :] + value
+            else:
+                mine[:, piece] = mine[:, piece] + value
+        store = pltpu.make_async_copy(mine, dst, s_out.at[u])
+        store.start()
+        stores.append(store)
+    for store in stores:
+        store.wait()
 
 
 def layer_call(sizes, *refs):
@@ -668,12 +700,14 @@
         in_specs=[vmem] + [hbm] * 6,
         out_specs=(hbm,) * 5,
         scratch_shapes=[
-            pltpu.VMEM((3, 3, third, width), F32),
+            pltpu.VMEM((2, count, width), BF16),
+            pltpu.VMEM((hidden, width), F32),
+            pltpu.VMEM((width, hidden), F32),
+            pltpu.VMEM((width, hidden), F32),
             pltpu.VMEM((3, 3, third, width), BF16),
-            dma((2,)),
-            dma((3, 3)),
-            dma((3, 3)),
-            dma((3, 3)),
+            dma((3, 2)),
+            dma((3,)),
+            dma((2, 2)),
         ],
         compiler_params=pltpu.CompilerParams(vmem_limit_bytes=58 * 1024 * 1024),
     )(paired.reshape(1, 1), *outs)

time: 181 us -> 176 us (0.972)
  Pallas kernels: 179 us -> 175 us
    pallas_call x1, Pallas kernels: 174 us -> 171 us  [per_device(): pl.pallas_call(functools.partial(layer_call, (n, n_exp, cap, lag, LATE)),...]
where the time goes in v3:
time: 176 us
  Pallas kernels  175 us (99%)
    pallas_call x1, Pallas kernels, per_device(): pl.pallas_call(functools.partial(layer_call, (n, n_exp, cap, lag, LATE)),...  171 us
    pallas_call x1, Pallas kernels, per_device(): pl.pallas_call(finish, out_shape=(jax.ShapeDtypeStruct((count, width), BF...  3.61 us

profile of v3, /device:TPU:8, one launch (start us, length us, event | category | flops | bytes accessed | tf_op | source)
XLA Modules:
  0.0 176.1 jit_solution(17317496193075315387)
XLA Ops:
  1.3 171.0 %shard_map.119 = (bf16[128,256]{1,0:T(8,128)(2,1)}, bf16[128,256]{1,0:T(8,128)(2,1)}, f32[768,256]{1,0:T(8,128)}, f32[256,768]{1,0:T(8,128)}, f32[256,768]{1,0:T(8,128)}, /*index=5*/bf16[3,3,256,256]{3,2,1,0:T(8,128)(2,1)}) custom-call(s32[8,128]{1,0:T(8,128)} %bitcast.13, f32[8,128]{1,0:T(8,128)} %bitcast.14, bf16[128,256]{1,0:T(8,128)(2,1)} %refs_2_.1, ...), custom_call_target="tpu_custom_call" | custom-call | tf_op jit(solution)/shard_map/pallas_call | solution.py:621
  172.3 3.6 %shard_map.120 = (bf16[128,256]{1,0:T(8,128)(2,1)}, bf16[128,256]{1,0:T(8,128)(2,1)}, f32[768,256]{1,0:T(8,128)}, f32[256,768]{1,0:T(8,128)}, f32[256,768]{1,0:T(8,128)}) custom-call(s32[1,1]{1,0:T(1,128)} %bitcast.9.paired, bf16[128,256]{1,0:T(8,128)(2,1)} %get-tuple-element.16.y_in, bf16[128,256]{1,0:T(8,128)(2,1)} %get-tuple-element.17.gt_in, ...), custom_call_target="tpu_custom_call" | custom-call | tf_op jit(solution)/shard_map/pallas_call | solution.py:691
